TPU v7x, 32 devices: a whole 2x2x4 slice. The times are simulated.
32 devices in a mesh: tm: 8 (over y, x, core), seq: 4 (over z).
Axes of the slice: x: 2, y: 2, z: 4, core: 2. Of those that a mesh axis runs over, the one named last changes fastest.
Arguments:
- latents: bfloat16 [32, 16, 2048], P('tm', None, 'seq'), may hold values from -6 to 6
- hidden: bfloat16 [16384, 3072], P(('tm', 'seq')), may hold values from -6 to 6
- grad_out: bfloat16 [32, 512, 2048], P('tm', None, 'seq'), may hold values from -6 to 6
- conv_in_w: bfloat16 [3, 512, 16], replicated, may hold values from -0.875 to 0.875
- conv_in_b: float32 [512], replicated, may hold values from -4 to 4
- conv_w: bfloat16 [3, 512, 512], replicated, may hold values from -0.15625 to 0.15625
- final_w: bfloat16 [3072, 64], replicated, may hold values from -0.109375 to 0.109375
- modulation: float32 [2, 3072], replicated, may hold values from -3 to 3
- clip_start: int32 [32], replicated, may hold values from 0 to 31, as said below
Outputs:
- hidden_input_gradient: bfloat16 [16384, 3072], P(('tm', 'seq'))
- convolution_weight_gradient: float32 [512, 3, 512], P(('tm', 'seq'))
- input_convolution_gradient: float32 [3, 512, 16], replicated
- input_bias_gradient: float32 [512], replicated
- final_grad: float32 [3072, 64], replicated
- modulation_grad: float32 [2, 3072], replicated
Inputs may be any that keep to these rules, and one draw needn't show every extreme that they name: Clips are consecutive runs of frames: clip_start never falls, clip_start[t] <= t, clip_start[t] == t at each clip's first frame; every clip has 9 to 33 frames except the last two, which are cut by the bin's end; the bin's last frame begins a clip of its own.
All inputs are finite; a program needn't handle non-finite values.
Results may differ from a plain program's by a relative error of at most 0.012.
Values may be sent and summed in bfloat16 or wider, within the bound.
A program may use at most 128 MiB of HBM per device.

v0:
```python
import functools

import jax
import jax.numpy as jnp
from jax import lax
from jax.experimental import pallas as pl
from jax.experimental.pallas import tpu as pltpu
from jax.sharding import PartitionSpec as P

F32 = jnp.float32
BF16 = jnp.bfloat16
MESH = pl.DeviceIdType.MESH
PATCH = 4
MAX_VMEM = 60 * 1024 * 1024


def dot(a, b, ca, cb):
    return lax.dot_general(a, b, (((ca,), (cb,)), ((), ())), preferred_element_type=F32)


def load_in_weights(w_in_ref, b_ref, w64):
    bias = b_ref[...]
    hi = bias.astype(BF16)
    mid = (bias - hi.astype(F32)).astype(BF16)
    lo = (bias - hi.astype(F32) - mid.astype(F32)).astype(BF16)
    pad = jnp.zeros((16 - 3, bias.shape[1]), F32)
    rows = jnp.concatenate(
        [w_in_ref[...].astype(F32), hi.astype(F32), mid.astype(F32), lo.astype(F32), pad], axis=0
    )
    w64[...] = rows.T.astype(BF16)


def load_window(prev_ref, lat_ref, latx):
    latx[: prev_ref.shape[0]] = prev_ref[...]
    latx[prev_ref.shape[0] :] = lat_ref[...]


def source(clip_ref, frame, tap):
    frames = clip_ref.shape[0]
    return jnp.maximum(frame - tap, clip_ref[jnp.clip(frame, 0, frames - 1)])


def pre_of(clip_ref, latx, z, w64, frame, base):
    cl = latx.shape[1]
    top = latx.shape[0] - 1
    for tap in range(3):
        row = jnp.clip(source(clip_ref, frame, tap) - base, 0, top)
        z[tap * cl : (tap + 1) * cl] = latx[row]
    z[3 * cl :] = jnp.ones_like(z[3 * cl :])
    return dot(w64[...], z[...], 1, 0)


def sigmoid(x):
    return 0.5 * jnp.tanh(0.5 * x) + 0.5


def weight_kernel(clip_ref, prev_ref, lat_ref, grad_ref, w_in_ref, b_ref, out_ref, latx, z, w64, act, acc):
    step = pl.program_id(0)
    slab = lat_ref.shape[0]
    halo = prev_ref.shape[0]
    chans = grad_ref.shape[1]
    first = lax.axis_index("tm") * slab

    def activate(frame):
        pre = pre_of(clip_ref, latx, z, w64, frame, first - halo)
        act[frame - first + 2] = (pre * sigmoid(pre)).astype(BF16)

    @pl.when(step == 0)
    def _():
        load_in_weights(w_in_ref, b_ref, w64)
        load_window(prev_ref, lat_ref, latx)
        acc[...] = jnp.zeros_like(acc)

    @pl.loop(jnp.where(step == 0, -2, step), step + 1)
    def _(t):
        activate(first + t)

    grad = grad_ref[0]
    for tap in range(3):
        row = source(clip_ref, first + step, tap) - first + 2
        acc[:, tap * chans : (tap + 1) * chans] += dot(grad, act[row], 1, 1)

    @pl.when(step == slab - 1)
    def _():
        n_tm, n_seq, rows, _ = out_ref.shape
        for i in range(n_tm):
            for j in range(n_seq):
                at = (i * n_seq + j) * rows
                out_ref[i, j] = acc[at : at + rows, :].astype(BF16)


def latent_kernel(
    clip_ref, prev_ref, lat_ref, grad_ref, next_ref, w_in_ref, b_ref, w_ref,
    lg_ref, misc_ref, latx, z, w64, wt, gx, sem,
):
    step = pl.program_id(0)
    slab = lat_ref.shape[0]
    halo = prev_ref.shape[0]
    chans = w_ref.shape[1]
    cl = lat_ref.shape[1]
    frames = clip_ref.shape[0]
    first = lax.axis_index("tm") * slab

    @pl.when(step == 0)
    def _():
        own = pltpu.make_async_copy(grad_ref, gx.at[pl.ds(0, slab * chans)], sem.at[0])
        own.start()
        following = pltpu.make_async_copy(next_ref, gx.at[pl.ds(slab * chans, 2 * chans)], sem.at[1])
        following.start()
        load_in_weights(w_in_ref, b_ref, w64)
        load_window(prev_ref, lat_ref, latx)
        for tap in range(3):
            wt[:, tap * chans : (tap + 1) * chans] = w_ref[tap].T
        lg_ref[...] = jnp.zeros_like(lg_ref)
        misc_ref[...] = jnp.zeros_like(misc_ref)
        own.wait()
        following.wait()

    s = first + step
    spare = (slab + 2) * chans

    def start_of(frame):
        return jnp.where(frame < frames, clip_ref[jnp.minimum(frame, frames - 1)], frames)

    a1 = start_of(s + 1) <= s
    a2 = start_of(s + 2) <= s
    b0 = start_of(s) == s
    b1 = start_of(s + 1) == s
    plain = a1 & a2 & jnp.logical_not(b0) & jnp.logical_not(b1)

    @pl.when(jnp.logical_not(plain))
    def _():
        g0 = gx[pl.ds(pl.multiple_of(step * chans, chans), chans)]
        g1 = gx[pl.ds(pl.multiple_of((step + 1) * chans, chans), chans)].astype(F32)
        g2 = gx[pl.ds(pl.multiple_of((step + 2) * chans, chans), chans)].astype(F32)
        gf = g0.astype(F32)
        m = [jnp.where(c, 1.0, 0.0).astype(F32) for c in (a1, a2, b0, b1)]
        gx[spare : spare + chans] = g0
        gx[spare + chans : spare + 2 * chans] = (m[0] * g1 + m[2] * gf).astype(BF16)
        gx[spare + 2 * chans : spare + 3 * chans] = (m[1] * g2 + m[3] * g1 + m[2] * gf).astype(BF16)

    at = pl.multiple_of(jnp.where(plain, step * chans, spare), chans)
    grad_act = dot(wt[...], gx[pl.ds(at, 3 * chans)], 1, 0)
    pre = pre_of(clip_ref, latx, z, w64, s, first - halo)
    sig = sigmoid(pre)
    grad_pre = (grad_act * (sig * (1.0 + pre * (1.0 - sig)))).astype(BF16)
    misc_ref[...] += dot(z[...], grad_pre, 1, 1)
    parts = dot(w_in_ref[...], grad_pre, 1, 0)
    for tap in range(3):
        row = source(clip_ref, s, tap) - first + 2
        lg_ref[row] += parts[tap * cl : (tap + 1) * cl]


def token_kernel(
    n_tm, n_seq,
    lg_ref, hid_ref, fw_ref, modu_ref, w4_ref, misc_ref,
    dx_ref, wg_ref, fin_ref, mod_ref, min_ref,
    tok, tok_halo, facc, macc, wrecv, wsum, wrecv2, f4, frecv, fsum, frecv2, gath,
    s_tok, r_tok, s_halo, r_halo, s_w, r_w, s_w2, r_w2, s_f, r_f, s_f2, r_f2, s_g, r_g, s_g2, r_g2,
):
    i = lax.axis_index("tm")
    j = lax.axis_index("seq")
    tms = [(d, lax.rem(i + d, n_tm)) for d in range(1, n_tm)]
    seqs = [(d, lax.rem(j + d, n_seq)) for d in range(1, n_seq)]
    cl = lg_ref.shape[1]
    width = lg_ref.shape[2]
    d_model = hid_ref.shape[1]
    takes_halo = (i < n_tm - 1) & (j >= n_seq - 2)

    barrier = pltpu.get_barrier_semaphore()
    for _, p in tms:
        pl.semaphore_signal(barrier, inc=1, device_id=(p, j), device_id_type=MESH)
    for _, p in seqs:
        pl.semaphore_signal(barrier, inc=1, device_id=(i, p), device_id_type=MESH)

    @pl.when(j >= n_seq - 2)
    def _():
        for p in range(n_seq):
            pl.semaphore_signal(barrier, inc=1, device_id=(lax.rem(i + 1, n_tm), p), device_id_type=MESH)

    pl.semaphore_wait(barrier, n_tm + n_seq)

    def copy(src, dst, send, recv, to):
        return pltpu.make_async_remote_copy(
            src_ref=src, dst_ref=dst, send_sem=send, recv_sem=recv, device_id=to, device_id_type=MESH
        )

    tok_copies = [
        copy(lg_ref.at[2 + p], tok.at[j], s_tok.at[d - 1], r_tok.at[d - 1], (i, p)) for d, p in seqs
    ]

    def halo_copy(h):
        return copy(lg_ref.at[h], tok_halo.at[j], s_halo.at[h], r_halo.at[j], (i - 1, n_seq - 2 + h))

    for c in tok_copies:
        c.start()

    @pl.when(i > 0)
    def _():
        for h in range(2):
            halo_copy(h).start()

    w_copies = [
        copy(w4_ref.at[p], wrecv.at[d - 1], s_w.at[d - 1], r_w.at[d - 1], (p, j)) for d, p in tms
    ]
    for c in w_copies:
        c.start()

    @pl.when(jnp.logical_not(takes_halo))
    def _():
        tok_halo[...] = jnp.zeros_like(tok_halo)

    n = width // PATCH
    row = lax.broadcasted_iota(jnp.int32, (width, width), 0)
    col = lax.broadcasted_iota(jnp.int32, (width, width), 1)
    spread = jnp.where(row == lax.rem(col, n) * PATCH + lax.div(col, n), 1.0, 0.0).astype(BF16)
    e = cl * PATCH
    row = lax.broadcasted_iota(jnp.int32, (e, e), 0)
    col = lax.broadcasted_iota(jnp.int32, (e, e), 1)
    order = jnp.where(row == lax.rem(col, cl) * PATCH + lax.div(col, cl), 1.0, 0.0).astype(BF16)

    facc[...] = jnp.zeros_like(facc)
    macc[...] = jnp.zeros_like(macc)
    for c in tok_copies:
        c.wait()

    @pl.when(i > 0)
    def _():
        for h in range(2):
            halo_copy(h).wait_send()

    @pl.when(takes_halo)
    def _():
        for p in range(n_seq):
            copy(lg_ref.at[0], tok_halo.at[p], s_halo.at[0], r_halo.at[p], (i, j)).wait_recv()

    tok[j] = lg_ref[2 + j]

    shift = modu_ref[0:1, :]
    scale = 1.0 + modu_ref[1:2, :]

    @pl.loop(0, n_seq)
    def _(r):
        lat = (tok[r] + tok_halo[r]).astype(BF16)
        split = dot(lat, spread, 1, 0)
        stack = jnp.concatenate([split[:, q * n : (q + 1) * n] for q in range(PATCH)], axis=0)
        tg_t = dot(order, stack.astype(BF16), 1, 0)
        tg = tg_t.T.astype(BF16)
        rows = pl.ds(pl.multiple_of(r * n, n), n)
        hid = hid_ref[rows, :].astype(F32)
        center = hid - jnp.mean(hid, axis=1, keepdims=True)
        inv = lax.rsqrt(jnp.mean(center * center, axis=1, keepdims=True) + 1e-06)
        normed = center * inv
        modulated = (normed * scale + shift).astype(BF16)
        facc[...] += dot(tg_t.astype(BF16), modulated, 1, 0)
        mod_in = dot(tg, fw_ref[...], 1, 0)
        macc[0:1] += jnp.sum(mod_in, axis=0, keepdims=True)
        macc[1:2] += jnp.sum(mod_in * normed, axis=0, keepdims=True)
        ng = mod_in * scale
        m1 = jnp.mean(ng, axis=1, keepdims=True)
        m2 = jnp.mean(ng * normed, axis=1, keepdims=True)
        dx_ref[rows, :] = (inv * (ng - m1 - normed * m2)).astype(BF16)

    chans = misc_ref.shape[1]
    wf = d_model // n_tm
    wm = chans // n_tm
    er = e // n_seq
    pieces = d_model // chans
    small = jnp.concatenate(
        [misc_ref[0 : 3 * cl + 1, :]]
        + [macc[b : b + 1, p * chans : (p + 1) * chans] for b in range(2) for p in range(pieces)]
        + [jnp.zeros((e - 3 * cl - 1 - 2 * pieces, chans), F32)],
        axis=0,
    )
    for a in range(n_tm):
        for b in range(n_seq):
            f4[a, b, :, :wf] = facc[b * er : (b + 1) * er, a * wf : (a + 1) * wf].astype(BF16)
            f4[a, b, :, wf : wf + wm] = small[b * er : (b + 1) * er, a * wm : (a + 1) * wm].astype(BF16)
            if wf + wm < f4.shape[3]:
                f4[a, b, :, wf + wm :] = jnp.zeros((er, f4.shape[3] - wf - wm), BF16)
    f_copies = [
        copy(f4.at[p], frecv.at[d - 1], s_f.at[d - 1], r_f.at[d - 1], (p, j)) for d, p in tms
    ]
    for c in f_copies:
        c.start()

    for c in w_copies:
        c.wait()
    for b in range(n_seq):
        total = w4_ref[i, b].astype(F32)
        for k in range(n_tm - 1):
            total = total + wrecv[k, b].astype(F32)
        wsum[b] = total.astype(BF16)
    w2_copies = [
        copy(wsum.at[p], wrecv2.at[d - 1], s_w2.at[d - 1], r_w2.at[d - 1], (i, p)) for d, p in seqs
    ]
    for c in w2_copies:
        c.start()

    for c in f_copies:
        c.wait()
    total = f4[i].astype(F32)
    for k in range(n_tm - 1):
        total = total + frecv[k].astype(F32)
    fsum[...] = total.astype(BF16)
    f2_copies = [
        copy(fsum.at[p], frecv2.at[d - 1], s_f2.at[d - 1], r_f2.at[d - 1], (i, p)) for d, p in seqs
    ]
    for c in f2_copies:
        c.start()

    for c in w2_copies:
        c.wait()
    total = wsum[j].astype(F32)
    for k in range(n_seq - 1):
        total = total + wrecv2[k].astype(F32)
    for tap in range(3):
        wg_ref[tap] = total[:, tap * chans : (tap + 1) * chans]

    for c in f2_copies:
        c.wait()
    total = fsum[j].astype(F32)
    for k in range(n_seq - 1):
        total = total + frecv2[k].astype(F32)
    gath[i, j] = total.astype(BF16)
    g_copies = [
        copy(gath.at[i, j], gath.at[i, j], s_g.at[d - 1], r_g.at[d - 1], (i, p)) for d, p in seqs
    ]
    for c in g_copies:
        c.start()
    for c in g_copies:
        c.wait()
    g2_copies = [
        copy(gath.at[i], gath.at[i], s_g2.at[d - 1], r_g2.at[d - 1], (p, j)) for d, p in tms
    ]
    for c in g2_copies:
        c.start()
    for c in g2_copies:
        c.wait()
    for a in range(n_tm):
        for b in range(n_seq):
            fin_ref[b * er : (b + 1) * er, a * wf : (a + 1) * wf] = gath[a, b, :, :wf].astype(F32)
            min_ref[b * er : (b + 1) * er, a * wm : (a + 1) * wm] = gath[a, b, :, wf : wf + wm].astype(F32)
    for b in range(2):
        for p in range(pieces):
            at = 3 * cl + 1 + b * pieces + p
            mod_ref[b : b + 1, p * chans : (p + 1) * chans] = min_ref[at : at + 1, :]


def local(n_tm, n_seq, latents, hidden, grad_out, conv_in_w, conv_in_b, conv_w, final_w, modulation, clip_start):
    slab, cl, width = latents.shape
    taps, chans = conv_w.shape[:2]
    tokens, d_model = hidden.shape
    rows = chans // (n_tm * n_seq)
    backward = [(k, k - 1) for k in range(1, n_tm)]
    forward = [(k, k + 1) for k in range(n_tm - 1)]
    lat_prev = lax.ppermute(latents[slab - 4 :], "tm", forward)
    grad_next = lax.ppermute(grad_out[:2], "tm", backward)
    w_in = conv_in_w.transpose(0, 2, 1).reshape(taps * cl, chans)
    bias = conv_in_b.reshape(1, chans)

    def whole(*shape):
        return pl.BlockSpec(shape, lambda t, c: (0,) * len(shape))

    window = [
        pltpu.VMEM((slab + 4, cl, width), BF16),
        pltpu.VMEM((4 * cl, width), BF16),
        pltpu.VMEM((chans, 4 * cl), BF16),
    ]
    w4 = pl.pallas_call(
        weight_kernel,
        out_shape=jax.ShapeDtypeStruct((n_tm, n_seq, rows, taps * chans), BF16),
        grid_spec=pltpu.PrefetchScalarGridSpec(
            num_scalar_prefetch=1,
            grid=(slab,),
            in_specs=[
                whole(4, cl, width),
                whole(slab, cl, width),
                pl.BlockSpec((1, chans, width), lambda t, c: (t, 0, 0)),
                whole(taps * cl, chans),
                whole(1, chans),
            ],
            out_specs=whole(n_tm, n_seq, rows, taps * chans),
            scratch_shapes=window
            + [pltpu.VMEM((slab + 2, chans, width), BF16), pltpu.VMEM((chans, taps * chans), F32)],
        ),
        compiler_params=pltpu.CompilerParams(vmem_limit_bytes=MAX_VMEM),
        cost_estimate=pl.CostEstimate(flops=7 * 10**9, bytes_accessed=6 * 10**6, transcendentals=2 * 10**6),
        name="weight_grad",
    )(clip_start, lat_prev, latents, grad_out, w_in, bias)

    lg, misc = pl.pallas_call(
        latent_kernel,
        out_shape=(
            jax.ShapeDtypeStruct((slab + 2, cl, width), F32),
            jax.ShapeDtypeStruct((4 * cl, chans), F32),
        ),
        grid_spec=pltpu.PrefetchScalarGridSpec(
            num_scalar_prefetch=1,
            grid=(slab,),
            in_specs=[
                whole(4, cl, width),
                whole(slab, cl, width),
                pl.BlockSpec(memory_space=pl.ANY),
                pl.BlockSpec(memory_space=pl.ANY),
                whole(taps * cl, chans),
                whole(1, chans),
                whole(taps, chans, chans),
            ],
            out_specs=(whole(slab + 2, cl, width), whole(4 * cl, chans)),
            scratch_shapes=window
            + [
                pltpu.VMEM((chans, taps * chans), BF16),
                pltpu.VMEM(((slab + 5) * chans, width), BF16),
                pltpu.SemaphoreType.DMA((2,)),
            ],
        ),
        compiler_params=pltpu.CompilerParams(vmem_limit_bytes=MAX_VMEM),
        cost_estimate=pl.CostEstimate(flops=7 * 10**9, bytes_accessed=6 * 10**6, transcendentals=10**6),
        name="latent_grad",
    )(
        clip_start, lat_prev, latents, grad_out.reshape(slab * chans, width),
        grad_next.reshape(2 * chans, width), w_in, bias, conv_w,
    )

    e = cl * PATCH
    er = e // n_seq
    cw = -(-((d_model + chans) // n_tm) // 128) * 128
    vmem = pl.BlockSpec(memory_space=pltpu.VMEM)
    dma = pltpu.SemaphoreType.DMA
    nt, ns = n_tm - 1, n_seq - 1
    dx, wg, fin, mod, small = pl.pallas_call(
        functools.partial(token_kernel, n_tm, n_seq),
        out_shape=(
            jax.ShapeDtypeStruct((tokens, d_model), BF16),
            jax.ShapeDtypeStruct((taps, rows, chans), F32),
            jax.ShapeDtypeStruct((e, d_model), F32),
            jax.ShapeDtypeStruct((2, d_model), F32),
            jax.ShapeDtypeStruct((e, chans), F32),
        ),
        in_specs=[vmem] * 6,
        out_specs=(vmem,) * 5,
        scratch_shapes=[
            pltpu.VMEM((n_seq, cl, width), F32),
            pltpu.VMEM((n_seq, cl, width), F32),
            pltpu.VMEM((e, d_model), F32),
            pltpu.VMEM((8, d_model), F32),
            pltpu.VMEM((nt, n_seq, rows, taps * chans), BF16),
            pltpu.VMEM((n_seq, rows, taps * chans), BF16),
            pltpu.VMEM((ns, rows, taps * chans), BF16),
            pltpu.VMEM((n_tm, n_seq, er, cw), BF16),
            pltpu.VMEM((nt, n_seq, er, cw), BF16),
            pltpu.VMEM((n_seq, er, cw), BF16),
            pltpu.VMEM((ns, er, cw), BF16),
            pltpu.VMEM((n_tm, n_seq, er, cw), BF16),
            dma((ns,)), dma((ns,)), dma((2,)), dma((n_seq,)),
            dma((nt,)), dma((nt,)), dma((ns,)), dma((ns,)),
            dma((nt,)), dma((nt,)), dma((ns,)), dma((ns,)),
            dma((ns,)), dma((ns,)), dma((nt,)), dma((nt,)),
        ],
        compiler_params=pltpu.CompilerParams(
            vmem_limit_bytes=MAX_VMEM, collective_id=0, has_side_effects=True
        ),
        name="token_grad",
    )(lg, hidden, final_w.T, modulation, w4, misc)
    return (
        dx,
        wg.transpose(1, 0, 2),
        small[: taps * cl].reshape(taps, cl, chans).transpose(0, 2, 1),
        small[taps * cl],
        fin.T,
        mod,
    )


def solution(mesh):
    return jax.shard_map(
        functools.partial(local, mesh.shape["tm"], mesh.shape["seq"]),
        mesh=mesh,
        in_specs=(
            P("tm", None, "seq"),
            P(("tm", "seq"), None),
            P("tm", None, "seq"),
            P(),
            P(),
            P(),
            P(),
            P(),
            P(),
        ),
        out_specs=(P(("tm", "seq"), None), P(("tm", "seq"), None, None), P(), P(), P(), P()),
        check_vma=False,
    )
```

profile of v0, /device:TPU:1, one launch (start us, length us, event | category | flops | bytes accessed | tf_op | source)
XLA Modules:
  0.0 92.6 jit_solution(13105739684971800063)
XLA Ops:
  0.6 1.3 %slice.9 = bf16[2,512,512]{2,1,0:T(8,128)(2,1)S(1)} slice(bf16[4,512,512]{2,1,0:T(8,128)(2,1)} %grad_ref.1), slice={[0:2], [0:512], [0:512]} | slice | bytes 2097152 | tf_op jit(solution)/shard_map/slice | solution.py:358
  1.9 1.9 %collective-permute-start.1 = (bf16[2,512,512]{2,1,0:T(8,128)(2,1)S(1)}, bf16[2,512,512]{2,1,0:T(8,128)(2,1)S(1)}, u32[]{:S(2)}, u32[]{:S(2)}) collective-permute-start(bf16[2,512,512]{2,1,0:T(8,128)(2,1)S(1)} %slice.9), channel_id=1, source_target_pairs={{4,0},{8,4},{12,8},{16,12},{20,16},{24,20},{28,24},{5,1},{9,5},{13... | collective-permute-start | bytes 3145736 | tf_op jit(solution)/shard_map/ppermute | solution.py:358
  3.9 4.5 %collective-permute-start = (bf16[4,16,512]{2,1,0:T(8,128)(2,1)}, bf16[4,16,512]{2,1,0:T(8,128)(2,1)S(1)}, u32[]{:S(2)}, u32[]{:S(2)}) collective-permute-start(bf16[4,16,512]{2,1,0:T(8,128)(2,1)} %lat_ref.3), channel_id=1, source_target_pairs={{0,4},{4,8},{8,12},{12,16},{16,20},{20,24},{24,28},{1,5},{5,9},{9,... | collective-permute-start | bytes 196616 | tf_op jit(solution)/shard_map/ppermute | solution.py:357
  8.4 1.6 %collective-permute-done.prev_ref = bf16[4,16,512]{2,1,0:T(8,128)(2,1)S(1)} collective-permute-done((bf16[4,16,512]{2,1,0:T(8,128)(2,1)}, bf16[4,16,512]{2,1,0:T(8,128)(2,1)S(1)}, u32[]{:S(2)}, u32[]{:S(2)}) %collective-permute-start) | collective-permute-done | bytes 65568 | tf_op jit(solution)/shard_map/ppermute | solution.py:357
  10.0 0.0 copy-start.4
  10.0 0.6 copy-done.4
  10.6 9.6 %weight_grad.1.w4_ref = bf16[8,4,16,1536]{3,2,1,0:T(8,128)(2,1)} custom-call(s32[32]{0:T(128)} %clip_ref.3, bf16[4,16,512]{2,1,0:T(8,128)(2,1)} %copy-done.4, bf16[4,16,512]{2,1,0:T(8,128)(2,1)} %lat_ref.3, bf16[4,512,512]{2,1,0:T(8,128)(2,1)} %grad_ref.1, bf16[48,512]{1,0:T(8,128)(2,1)} %bitcast.20, f32[1,512]{1,0:T(1,128)} %bitcast.22), custom_call_target="tpu_custom_call" | custom-call | flops 7000000000 | bytes 6000000 | tf_op jit(solution)/shard_map/weight_grad/pallas_call | solution.py:370
  20.2 0.0 collective-permute-done.1
  20.2 0.0 copy-start.3
  20.2 1.0 %copy-done.3 = bf16[2,512,512]{2,1,0:T(8,128)(2,1)} copy-done((bf16[2,512,512]{2,1,0:T(8,128)(2,1)}, bf16[2,512,512]{2,1,0:T(8,128)(2,1)S(1)}, u32[]{:S(2)}) %copy-start.3) | copy-done | bytes 1048600
  21.1 11.3 %latent_grad.1 = (f32[6,16,512]{2,1,0:T(8,128)}, f32[64,512]{1,0:T(8,128)}) custom-call(s32[32]{0:T(128)} %clip_ref.3, bf16[4,16,512]{2,1,0:T(8,128)(2,1)} %copy-done.4, bf16[4,16,512]{2,1,0:T(8,128)(2,1)} %lat_ref.3, bf16[2048,512]{1,0:T(8,128)(2,1)} %bitcast.14, bf16[1024,512]{1,0:T(8,128)(2,1)} %bitcast.19, bf16[48,512]{1,0:T(8,128)(2,1)} %bitcast.21, ...), custom_call_target="tpu_custom_call" | custom-call | flops 7000000000 | bytes 6000000 | tf_op jit(solution)/shard_map/latent_grad/pallas_call | solution.py:392
  32.5 51.3 %token_grad.1 = (bf16[512,3072]{1,0:T(8,128)(2,1)}, f32[3,16,512]{2,1,0:T(8,128)}, f32[64,3072]{1,0:T(8,128)}, f32[2,3072]{1,0:T(2,128)}, f32[64,512]{1,0:T(8,128)}) custom-call(f32[6,16,512]{2,1,0:T(8,128)} %get-tuple-element.13.lg_ref, bf16[512,3072]{1,0:T(8,128)(2,1)} %hid_ref.1, bf16[64,3072]{1,0:T(8,128)(2,1)} %bitcast.15, f32[2,3072]{1,0:T(2,128)} %modu_ref.1, ...), custom_call_target="tpu_custom_call" | custom-call | tf_op jit(solution)/shard_map/token_grad/pallas_call | solution.py:432
  83.8 1.5 %slice.10 = f32[48,512]{1,0:T(8,128)} slice(f32[64,512]{1,0:T(8,128)} %get-tuple-element.17), slice={[0:48], [0:512]} | slice | bytes 196608 | tf_op jit(solution)/shard_map/slice | solution.py:469
  85.4 1.3 %slice.11 = f32[1,512]{1,0:T(1,128)} slice(f32[64,512]{1,0:T(8,128)} %get-tuple-element.17), slice={[48:49], [0:512]} | slice | bytes 4096 | tf_op jit(solution)/shard_map/slice | solution.py:470
  86.6 0.0 copy-start.1
  86.6 0.0 copy-start
  86.7 0.0 copy-start.2
  86.7 3.8 %copy.19 = bf16[512,3072]{1,0:T(8,128)(2,1)} copy(bf16[512,3072]{1,0:T(8,128)(2,1)} %get-tuple-element.26) | data formatting | bytes 6291456
  90.5 0.0 copy-done.1
  90.5 0.6 copy.20
  91.1 0.0 copy-done
  91.1 0.9 copy.21
  92.0 0.0 copy-done.2
  92.0 0.6 copy.22
Async XLA Ops:
  1.9 18.2 %collective-permute-start.1 = (bf16[2,512,512]{2,1,0:T(8,128)(2,1)S(1)}, bf16[2,512,512]{2,1,0:T(8,128)(2,1)S(1)}, u32[]{:S(2)}, u32[]{:S(2)}) collective-permute-start(bf16[2,512,512]{2,1,0:T(8,128)(2,1)S(1)} %slice.9), channel_id=1, source_target_pairs={{4,0},{8,4},{12,8},{16,12},{20,16},{24,20},{28,24},{5,1},{9,5},{13... | collective-permute-start | bytes 3145736 | tf_op jit(solution)/shard_map/ppermute | solution.py:358
  3.9 6.1 %collective-permute-start = (bf16[4,16,512]{2,1,0:T(8,128)(2,1)}, bf16[4,16,512]{2,1,0:T(8,128)(2,1)S(1)}, u32[]{:S(2)}, u32[]{:S(2)}) collective-permute-start(bf16[4,16,512]{2,1,0:T(8,128)(2,1)} %lat_ref.3), channel_id=1, source_target_pairs={{0,4},{4,8},{8,12},{12,16},{16,20},{20,24},{24,28},{1,5},{5,9},{9,... | collective-permute-start | bytes 196616 | tf_op jit(solution)/shard_map/ppermute | solution.py:357
  10.0 0.6 copy-start.4
  20.2 1.0 %copy-start.3 = (bf16[2,512,512]{2,1,0:T(8,128)(2,1)}, bf16[2,512,512]{2,1,0:T(8,128)(2,1)S(1)}, u32[]{:S(2)}) copy-start(bf16[2,512,512]{2,1,0:T(8,128)(2,1)S(1)} %collective-permute-done.1) | copy-start | bytes 3145732
  86.6 3.8 %copy-start.1 = (f32[3,16,512]{2,1,0:T(8,128)S(1)}, f32[3,16,512]{2,1,0:T(8,128)}, u32[]{:S(2)}) copy-start(f32[3,16,512]{2,1,0:T(8,128)} %get-tuple-element.16) | copy-start | bytes 294916
  86.6 4.5 %copy-start = (f32[64,3072]{1,0:T(8,128)S(1)}, f32[64,3072]{1,0:T(8,128)}, u32[]{:S(2)}) copy-start(f32[64,3072]{1,0:T(8,128)} %get-tuple-element.18) | copy-start | bytes 2359300
  86.7 5.4 %copy-start.2 = (f32[2,3072]{1,0:T(2,128)S(1)}, f32[2,3072]{1,0:T(2,128)}, u32[]{:S(2)}) copy-start(f32[2,3072]{1,0:T(2,128)} %get-tuple-element.31) | copy-start | bytes 73732
where the time goes:
time: 92.9 us; the launch traced here: 92.6 us
  Pallas kernels  72.2 us (78%)
  local copies, waits for them, and re-layouts  11.7 us (13%)
  starting transfers between devices  6.42 us (7%)
  waiting for transfers between devices  1.63 us (2%)
    pallas_call x1, Pallas kernels, local(): pl.pallas_call(functools.partial(token_kernel, n_tm, n_seq), out_shape=(j...  51.3 us
    pallas_call x1, Pallas kernels, local(): pl.pallas_call(latent_kernel, out_shape=(jax.ShapeDtypeStruct((slab + 2,...  11.3 us
    pallas_call x1, Pallas kernels, local(): pl.pallas_call(weight_kernel, out_shape=jax.ShapeDtypeStruct((n_tm, n_seq...  9.55 us
    unnamed x14, local copies, waits for them, and re-layouts  7.57 us
    ppermute x1, starting transfers between devices, local(): lat_prev = lax.ppermute(latents[slab - 4:], 'tm', forward)  4.49 us
    ppermute x1, starting transfers between devices, local(): grad_next = lax.ppermute(grad_out[:2], 'tm', backward)  1.93 us
  transfers between devices with their start and end apart: 2, of which 1 were waited for; matrix products, arithmetic and copies ran while one was open for 0% of the time, Pallas kernels for 10%

commit v1 on v0

--- a/solution.py
+++ b/solution.py
@@ -154,8 +154,8 @@
 def token_kernel(
     n_tm, n_seq,
     lg_ref, hid_ref, fw_ref, modu_ref, w4_ref, misc_ref,
-    dx_ref, wg_ref, fin_ref, mod_ref, min_ref,
-    tok, tok_halo, facc, macc, wrecv, wsum, wrecv2, f4, frecv, fsum, frecv2, gath,
+    dx_ref, wg_ref, gath,
+    tok, tok_halo, tgs, tcol, facc, macc, wrecv, wsum, wrecv2, f4, frecv, fsum, frecv2,
     s_tok, r_tok, s_halo, r_halo, s_w, r_w, s_w2, r_w2, s_f, r_f, s_f2, r_f2, s_g, r_g, s_g2, r_g2,
 ):
     i = lax.axis_index("tm")
@@ -220,7 +220,7 @@
     order = jnp.where(row == lax.rem(col, cl) * PATCH + lax.div(col, cl), 1.0, 0.0).astype(BF16)
 
     facc[...] = jnp.zeros_like(facc)
-    macc[...] = jnp.zeros_like(macc)
+    tcol[...] = jnp.zeros_like(tcol)
     for c in tok_copies:
         c.wait()
 
@@ -238,6 +238,15 @@
 
     shift = modu_ref[0:1, :]
     scale = 1.0 + modu_ref[1:2, :]
+
+    def rows_of(r):
+        return pl.ds(pl.multiple_of(r * n, n), n)
+
+    def normalise(r):
+        hid = hid_ref[rows_of(r), :].astype(F32)
+        center = hid - jnp.mean(hid, axis=1, keepdims=True)
+        inv = lax.rsqrt(jnp.mean(center * center, axis=1, keepdims=True) + 1e-06)
+        return center * inv, inv
 
     @pl.loop(0, n_seq)
     def _(r):
@@ -245,21 +254,16 @@
         split = dot(lat, spread, 1, 0)
         stack = jnp.concatenate([split[:, q * n : (q + 1) * n] for q in range(PATCH)], axis=0)
         tg_t = dot(order, stack.astype(BF16), 1, 0)
-        tg = tg_t.T.astype(BF16)
-        rows = pl.ds(pl.multiple_of(r * n, n), n)
-        hid = hid_ref[rows, :].astype(F32)
-        center = hid - jnp.mean(hid, axis=1, keepdims=True)
-        inv = lax.rsqrt(jnp.mean(center * center, axis=1, keepdims=True) + 1e-06)
-        normed = center * inv
-        modulated = (normed * scale + shift).astype(BF16)
-        facc[...] += dot(tg_t.astype(BF16), modulated, 1, 0)
-        mod_in = dot(tg, fw_ref[...], 1, 0)
-        macc[0:1] += jnp.sum(mod_in, axis=0, keepdims=True)
-        macc[1:2] += jnp.sum(mod_in * normed, axis=0, keepdims=True)
-        ng = mod_in * scale
-        m1 = jnp.mean(ng, axis=1, keepdims=True)
-        m2 = jnp.mean(ng * normed, axis=1, keepdims=True)
-        dx_ref[rows, :] = (inv * (ng - m1 - normed * m2)).astype(BF16)
+        tgs[rows_of(r), :] = tg_t.T.astype(BF16)
+        normed, _ = normalise(r)
+        facc[...] += dot(tg_t.astype(BF16), normed.astype(BF16), 1, 0)
+        tcol[...] += jnp.broadcast_to(jnp.sum(tg_t, axis=1, keepdims=True), tcol.shape)
+
+    column = tcol[:, 0:1]
+    fw = fw_ref[...].astype(F32)
+    macc[0:1] = jnp.sum(fw * column, axis=0, keepdims=True)
+    macc[1:2] = jnp.sum(fw * facc[...], axis=0, keepdims=True)
+    facc[...] = facc[...] * scale + column * shift
 
     chans = misc_ref.shape[1]
     wf = d_model // n_tm
@@ -284,6 +288,14 @@
     for c in f_copies:
         c.start()
 
+    @pl.loop(0, n_seq)
+    def _(r):
+        normed, inv = normalise(r)
+        ng = dot(tgs[rows_of(r), :], fw_ref[...], 1, 0) * scale
+        m1 = jnp.mean(ng, axis=1, keepdims=True)
+        m2 = jnp.mean(ng * normed, axis=1, keepdims=True)
+        dx_ref[rows_of(r), :] = (inv * (ng - m1 - normed * m2)).astype(BF16)
+
     for c in w_copies:
         c.wait()
     for b in range(n_seq):
@@ -337,14 +349,26 @@
         c.start()
     for c in g2_copies:
         c.wait()
+
+
+def unpack_kernel(gath, wg_ref, fin_ref, mod_ref, in_ref, bias_ref, wg_out, small):
+    n_tm, n_seq, er, _ = gath.shape
+    d_model = fin_ref.shape[1]
+    taps_cl, chans = in_ref.shape
+    wf = d_model // n_tm
+    wm = chans // n_tm
+    pieces = d_model // chans
     for a in range(n_tm):
         for b in range(n_seq):
             fin_ref[b * er : (b + 1) * er, a * wf : (a + 1) * wf] = gath[a, b, :, :wf].astype(F32)
-            min_ref[b * er : (b + 1) * er, a * wm : (a + 1) * wm] = gath[a, b, :, wf : wf + wm].astype(F32)
+            small[b * er : (b + 1) * er, a * wm : (a + 1) * wm] = gath[a, b, :, wf : wf + wm].astype(F32)
+    in_ref[...] = small[:taps_cl, :]
+    bias_ref[...] = small[taps_cl : taps_cl + 1, :]
     for b in range(2):
         for p in range(pieces):
-            at = 3 * cl + 1 + b * pieces + p
-            mod_ref[b : b + 1, p * chans : (p + 1) * chans] = min_ref[at : at + 1, :]
+            at = taps_cl + 1 + b * pieces + p
+            mod_ref[b : b + 1, p * chans : (p + 1) * chans] = small[at : at + 1, :]
+    wg_out[...] = wg_ref[...]
 
 
 def local(n_tm, n_seq, latents, hidden, grad_out, conv_in_w, conv_in_b, conv_w, final_w, modulation, clip_start):
@@ -429,20 +453,20 @@
     vmem = pl.BlockSpec(memory_space=pltpu.VMEM)
     dma = pltpu.SemaphoreType.DMA
     nt, ns = n_tm - 1, n_seq - 1
-    dx, wg, fin, mod, small = pl.pallas_call(
+    dx, wg, gath = pl.pallas_call(
         functools.partial(token_kernel, n_tm, n_seq),
         out_shape=(
             jax.ShapeDtypeStruct((tokens, d_model), BF16),
             jax.ShapeDtypeStruct((taps, rows, chans), F32),
-            jax.ShapeDtypeStruct((e, d_model), F32),
-            jax.ShapeDtypeStruct((2, d_model), F32),
-            jax.ShapeDtypeStruct((e, chans), F32),
+            jax.ShapeDtypeStruct((n_tm, n_seq, er, cw), BF16),
         ),
         in_specs=[vmem] * 6,
-        out_specs=(vmem,) * 5,
+        out_specs=(vmem,) * 3,
         scratch_shapes=[
             pltpu.VMEM((n_seq, cl, width), F32),
             pltpu.VMEM((n_seq, cl, width), F32),
+            pltpu.VMEM((tokens, e), BF16),
+            pltpu.VMEM((e, 128), F32),
             pltpu.VMEM((e, d_model), F32),
             pltpu.VMEM((8, d_model), F32),
             pltpu.VMEM((nt, n_seq, rows, taps * chans), BF16),
@@ -452,7 +476,6 @@
             pltpu.VMEM((nt, n_seq, er, cw), BF16),
             pltpu.VMEM((n_seq, er, cw), BF16),
             pltpu.VMEM((ns, er, cw), BF16),
-            pltpu.VMEM((n_tm, n_seq, er, cw), BF16),
             dma((ns,)), dma((ns,)), dma((2,)), dma((n_seq,)),
             dma((nt,)), dma((nt,)), dma((ns,)), dma((ns,)),
             dma((nt,)), dma((nt,)), dma((ns,)), dma((ns,)),
@@ -463,11 +486,25 @@
         ),
         name="token_grad",
     )(lg, hidden, final_w.T, modulation, w4, misc)
+    fin, mod, w_in_grad, bias_grad, wg = pl.pallas_call(
+        unpack_kernel,
+        out_shape=(
+            jax.ShapeDtypeStruct((e, d_model), F32),
+            jax.ShapeDtypeStruct((2, d_model), F32),
+            jax.ShapeDtypeStruct((taps * cl, chans), F32),
+            jax.ShapeDtypeStruct((1, chans), F32),
+            jax.ShapeDtypeStruct((taps, rows, chans), F32),
+        ),
+        in_specs=[vmem] * 2,
+        out_specs=(vmem,) * 5,
+        scratch_shapes=[pltpu.VMEM((e, chans), F32)],
+        name="unpack",
+    )(gath, wg)
     return (
         dx,
         wg.transpose(1, 0, 2),
-        small[: taps * cl].reshape(taps, cl, chans).transpose(0, 2, 1),
-        small[taps * cl],
+        w_in_grad.reshape(taps, cl, chans).transpose(0, 2, 1),
+        bias_grad.reshape(chans),
         fin.T,
         mod,
     )

time: 92.9 us -> 90.3 us (0.972)
  local copies, waits for them, and re-layouts: 11.7 us -> 6.65 us
  Pallas kernels: 72.2 us -> 75.1 us
    slice x2 -> x0, local copies, waits for them, and re-layouts: 2.84 us -> none  [the longest x1 1.54 us: local(): small[:taps * cl].reshape(taps, cl, chans).transpose(0, 2, 1)]
    unnamed x14 -> x5, local copies, waits for them, and re-layouts: 7.57 us -> 5.36 us
    pallas_call x0 -> x1, Pallas kernels: none -> 2.07 us  [local(): pl.pallas_call(unpack_kernel, out_shape=(jax.ShapeDtypeStruct((e, d_model...]
  transfers between devices with their start and end apart: 2 -> 2, of which waited for: 1 -> 1; matrix products, arithmetic and copies ran while one was open for 0% -> 0% of each run, Pallas kernels for 10% -> 11%
where the time goes in v1:
time: 90.3 us; the launch traced here: 90.4 us
  Pallas kernels  75.1 us (83%)
  local copies, waits for them, and re-layouts  6.65 us (7%)
  starting transfers between devices  6.42 us (7%)
  waiting for transfers between devices  1.63 us (2%)
    pallas_call x1, Pallas kernels, local(): pl.pallas_call(functools.partial(token_kernel, n_tm, n_seq), out_shape=(j...  52.1 us
    pallas_call x1, Pallas kernels, local(): pl.pallas_call(latent_kernel, out_shape=(jax.ShapeDtypeStruct((slab + 2,...  11.3 us
    pallas_call x1, Pallas kernels, local(): pl.pallas_call(weight_kernel, out_shape=jax.ShapeDtypeStruct((n_tm, n_seq...  9.55 us
    unnamed x5, local copies, waits for them, and re-layouts  5.36 us
    ppermute x1, starting transfers between devices, local(): lat_prev = lax.ppermute(latents[slab - 4:], 'tm', forward)  4.49 us
    pallas_call x1, Pallas kernels, local(): pl.pallas_call(unpack_kernel, out_shape=(jax.ShapeDtypeStruct((e, d_model...  2.07 us
    ppermute x1, starting transfers between devices, local(): grad_next = lax.ppermute(grad_out[:2], 'tm', backward)  1.93 us
  transfers between devices with their start and end apart: 2, of which 1 were waited for; matrix products, arithmetic and copies ran while one was open for 0% of the time, Pallas kernels for 11%

profile of v1, /device:TPU:1, one launch (start us, length us, event | category | flops | bytes accessed | tf_op | source)
XLA Modules:
  0.0 90.4 jit_solution(13073515804906580353)
XLA Ops:
  0.6 1.3 %slice.3 = bf16[2,512,512]{2,1,0:T(8,128)(2,1)S(1)} slice(bf16[4,512,512]{2,1,0:T(8,128)(2,1)} %grad_ref.1), slice={[0:2], [0:512], [0:512]} | slice | bytes 2097152 | tf_op jit(solution)/shard_map/slice | solution.py:382
  1.9 1.9 %collective-permute-start.1 = (bf16[2,512,512]{2,1,0:T(8,128)(2,1)S(1)}, bf16[2,512,512]{2,1,0:T(8,128)(2,1)S(1)}, u32[]{:S(2)}, u32[]{:S(2)}) collective-permute-start(bf16[2,512,512]{2,1,0:T(8,128)(2,1)S(1)} %slice.3), channel_id=1, source_target_pairs={{4,0},{8,4},{12,8},{16,12},{20,16},{24,20},{28,24},{5,1},{9,5},{13... | collective-permute-start | bytes 3145736 | tf_op jit(solution)/shard_map/ppermute | solution.py:382
  3.9 4.5 %collective-permute-start = (bf16[4,16,512]{2,1,0:T(8,128)(2,1)}, bf16[4,16,512]{2,1,0:T(8,128)(2,1)S(1)}, u32[]{:S(2)}, u32[]{:S(2)}) collective-permute-start(bf16[4,16,512]{2,1,0:T(8,128)(2,1)} %lat_ref.3), channel_id=1, source_target_pairs={{0,4},{4,8},{8,12},{12,16},{16,20},{20,24},{24,28},{1,5},{5,9},{9,... | collective-permute-start | bytes 196616 | tf_op jit(solution)/shard_map/ppermute | solution.py:381
  8.4 1.6 %collective-permute-done.prev_ref = bf16[4,16,512]{2,1,0:T(8,128)(2,1)S(1)} collective-permute-done((bf16[4,16,512]{2,1,0:T(8,128)(2,1)}, bf16[4,16,512]{2,1,0:T(8,128)(2,1)S(1)}, u32[]{:S(2)}, u32[]{:S(2)}) %collective-permute-start) | collective-permute-done | bytes 65568 | tf_op jit(solution)/shard_map/ppermute | solution.py:381
  10.0 0.0 copy-start.1
  10.0 0.6 copy-done.1
  10.6 9.6 %weight_grad.1.w4_ref = bf16[8,4,16,1536]{3,2,1,0:T(8,128)(2,1)} custom-call(s32[32]{0:T(128)} %clip_ref.3, bf16[4,16,512]{2,1,0:T(8,128)(2,1)} %copy-done.1, bf16[4,16,512]{2,1,0:T(8,128)(2,1)} %lat_ref.3, bf16[4,512,512]{2,1,0:T(8,128)(2,1)} %grad_ref.1, bf16[48,512]{1,0:T(8,128)(2,1)} %bitcast.19, f32[1,512]{1,0:T(1,128)} %bitcast.21), custom_call_target="tpu_custom_call" | custom-call | flops 7000000000 | bytes 6000000 | tf_op jit(solution)/shard_map/weight_grad/pallas_call | solution.py:394
  20.2 0.0 collective-permute-done.1
  20.2 0.0 copy-start
  20.2 1.0 %copy-done = bf16[2,512,512]{2,1,0:T(8,128)(2,1)} copy-done((bf16[2,512,512]{2,1,0:T(8,128)(2,1)}, bf16[2,512,512]{2,1,0:T(8,128)(2,1)S(1)}, u32[]{:S(2)}) %copy-start) | copy-done | bytes 1048600
  21.1 11.3 %latent_grad.1 = (f32[6,16,512]{2,1,0:T(8,128)}, f32[64,512]{1,0:T(8,128)}) custom-call(s32[32]{0:T(128)} %clip_ref.3, bf16[4,16,512]{2,1,0:T(8,128)(2,1)} %copy-done.1, bf16[4,16,512]{2,1,0:T(8,128)(2,1)} %lat_ref.3, bf16[2048,512]{1,0:T(8,128)(2,1)} %bitcast.13, bf16[1024,512]{1,0:T(8,128)(2,1)} %bitcast.15, bf16[48,512]{1,0:T(8,128)(2,1)} %bitcast.20, ...), custom_call_target="tpu_custom_call" | custom-call | flops 7000000000 | bytes 6000000 | tf_op jit(solution)/shard_map/latent_grad/pallas_call | solution.py:416
  32.5 52.1 %token_grad.1 = (bf16[512,3072]{1,0:T(8,128)(2,1)}, f32[3,16,512]{2,1,0:T(8,128)}, bf16[8,4,16,512]{3,2,1,0:T(8,128)(2,1)}) custom-call(f32[6,16,512]{2,1,0:T(8,128)} %get-tuple-element.16.lg_ref, bf16[512,3072]{1,0:T(8,128)(2,1)} %hid_ref.1, bf16[64,3072]{1,0:T(8,128)(2,1)} %bitcast.14, f32[2,3072]{1,0:T(2,128)} %modu_ref.1, ...), custom_call_target="tpu_custom_call" | custom-call | tf_op jit(solution)/shard_map/token_grad/pallas_call | solution.py:456
  84.6 2.1 %unpack.1 = (f32[64,3072]{1,0:T(8,128)}, f32[2,3072]{1,0:T(2,128)}, f32[48,512]{1,0:T(8,128)}, f32[1,512]{1,0:T(1,128)}, f32[3,16,512]{2,1,0:T(8,128)}) custom-call(bf16[8,4,16,512]{3,2,1,0:T(8,128)(2,1)} %get-tuple-element.19.gath, f32[3,16,512]{2,1,0:T(8,128)} %get-tuple-element.20.wg_ref), custom_call_target="tpu_custom_call" | custom-call | tf_op jit(solution)/shard_map/unpack/pallas_call | solution.py:489
  86.7 3.8 %copy.16 = bf16[512,3072]{1,0:T(8,128)(2,1)} copy(bf16[512,3072]{1,0:T(8,128)(2,1)} %get-tuple-element.32) | data formatting | bytes 6291456
Async XLA Ops:
  1.9 18.2 %collective-permute-start.1 = (bf16[2,512,512]{2,1,0:T(8,128)(2,1)S(1)}, bf16[2,512,512]{2,1,0:T(8,128)(2,1)S(1)}, u32[]{:S(2)}, u32[]{:S(2)}) collective-permute-start(bf16[2,512,512]{2,1,0:T(8,128)(2,1)S(1)} %slice.3), channel_id=1, source_target_pairs={{4,0},{8,4},{12,8},{16,12},{20,16},{24,20},{28,24},{5,1},{9,5},{13... | collective-permute-start | bytes 3145736 | tf_op jit(solution)/shard_map/ppermute | solution.py:382
  3.9 6.1 %collective-permute-start = (bf16[4,16,512]{2,1,0:T(8,128)(2,1)}, bf16[4,16,512]{2,1,0:T(8,128)(2,1)S(1)}, u32[]{:S(2)}, u32[]{:S(2)}) collective-permute-start(bf16[4,16,512]{2,1,0:T(8,128)(2,1)} %lat_ref.3), channel_id=1, source_target_pairs={{0,4},{4,8},{8,12},{12,16},{16,20},{20,24},{24,28},{1,5},{5,9},{9,... | collective-permute-start | bytes 196616 | tf_op jit(solution)/shard_map/ppermute | solution.py:381
  10.0 0.6 copy-start.1
  20.2 1.0 %copy-start = (bf16[2,512,512]{2,1,0:T(8,128)(2,1)}, bf16[2,512,512]{2,1,0:T(8,128)(2,1)S(1)}, u32[]{:S(2)}) copy-start(bf16[2,512,512]{2,1,0:T(8,128)(2,1)S(1)} %collective-permute-done.1) | copy-start | bytes 3145732

commit v2 on v1

--- a/solution.py
+++ b/solution.py
@@ -11,6 +11,7 @@
 BF16 = jnp.bfloat16
 MESH = pl.DeviceIdType.MESH
 PATCH = 4
+CORES = 2
 MAX_VMEM = 60 * 1024 * 1024
 
 
@@ -82,11 +83,11 @@
 
     @pl.when(step == slab - 1)
     def _():
-        n_tm, n_seq, rows, _ = out_ref.shape
-        for i in range(n_tm):
+        cores, chips, n_seq, rows, _ = out_ref.shape
+        for i in range(cores * chips):
             for j in range(n_seq):
                 at = (i * n_seq + j) * rows
-                out_ref[i, j] = acc[at : at + rows, :].astype(BF16)
+                out_ref[i % cores, i // cores, j] = acc[at : at + rows, :].astype(BF16)
 
 
 def latent_kernel(
@@ -155,12 +156,17 @@
     n_tm, n_seq,
     lg_ref, hid_ref, fw_ref, modu_ref, w4_ref, misc_ref,
     dx_ref, wg_ref, gath,
-    tok, tok_halo, tgs, tcol, facc, macc, wrecv, wsum, wrecv2, f4, frecv, fsum, frecv2,
-    s_tok, r_tok, s_halo, r_halo, s_w, r_w, s_w2, r_w2, s_f, r_f, s_f2, r_f2, s_g, r_g, s_g2, r_g2,
+    tok, tok_halo, tgs, tcol, facc, macc, wcore, whalf, wrecv, wsum, wrecv2, f4, fcore, fhalf, frecv, fsum, frecv2,
+    s_tok, r_tok, s_halo, r_halo, s_w, r_w, s_w2, r_w2, s_f, r_f, s_f2, r_f2, s_g, r_g, s_g2, r_g2, s_core, r_core,
 ):
     i = lax.axis_index("tm")
     j = lax.axis_index("seq")
-    tms = [(d, lax.rem(i + d, n_tm)) for d in range(1, n_tm)]
+    chips = n_tm // CORES
+    core = lax.rem(i, CORES)
+    chip = lax.div(i, CORES)
+    other = CORES - 1 - core
+    sibling = (chip * CORES + other, j)
+    tms = [(d, lax.rem(chip + d, chips)) for d in range(1, chips)]
     seqs = [(d, lax.rem(j + d, n_seq)) for d in range(1, n_seq)]
     cl = lg_ref.shape[1]
     width = lg_ref.shape[2]
@@ -169,7 +175,8 @@
 
     barrier = pltpu.get_barrier_semaphore()
     for _, p in tms:
-        pl.semaphore_signal(barrier, inc=1, device_id=(p, j), device_id_type=MESH)
+        pl.semaphore_signal(barrier, inc=1, device_id=(p * CORES + core, j), device_id_type=MESH)
+    pl.semaphore_signal(barrier, inc=1, device_id=sibling, device_id_type=MESH)
     for _, p in seqs:
         pl.semaphore_signal(barrier, inc=1, device_id=(i, p), device_id_type=MESH)
 
@@ -178,7 +185,7 @@
         for p in range(n_seq):
             pl.semaphore_signal(barrier, inc=1, device_id=(lax.rem(i + 1, n_tm), p), device_id_type=MESH)
 
-    pl.semaphore_wait(barrier, n_tm + n_seq)
+    pl.semaphore_wait(barrier, chips + n_seq + 1)
 
     def copy(src, dst, send, recv, to):
         return pltpu.make_async_remote_copy(
@@ -200,11 +207,8 @@
         for h in range(2):
             halo_copy(h).start()
 
-    w_copies = [
-        copy(w4_ref.at[p], wrecv.at[d - 1], s_w.at[d - 1], r_w.at[d - 1], (p, j)) for d, p in tms
-    ]
-    for c in w_copies:
-        c.start()
+    w_core = copy(w4_ref.at[other], wcore, s_core.at[0], r_core.at[0], sibling)
+    w_core.start()
 
     @pl.when(jnp.logical_not(takes_halo))
     def _():
@@ -221,6 +225,15 @@
 
     facc[...] = jnp.zeros_like(facc)
     tcol[...] = jnp.zeros_like(tcol)
+    w_core.wait()
+    for q in range(chips):
+        whalf[q] = (w4_ref[core, q].astype(F32) + wcore[q].astype(F32)).astype(BF16)
+    w_copies = [
+        copy(whalf.at[p], wrecv.at[d - 1], s_w.at[d - 1], r_w.at[d - 1], (p * CORES + core, j))
+        for d, p in tms
+    ]
+    for c in w_copies:
+        c.start()
     for c in tok_copies:
         c.wait()
 
@@ -278,29 +291,37 @@
     )
     for a in range(n_tm):
         for b in range(n_seq):
-            f4[a, b, :, :wf] = facc[b * er : (b + 1) * er, a * wf : (a + 1) * wf].astype(BF16)
-            f4[a, b, :, wf : wf + wm] = small[b * er : (b + 1) * er, a * wm : (a + 1) * wm].astype(BF16)
-            if wf + wm < f4.shape[3]:
-                f4[a, b, :, wf + wm :] = jnp.zeros((er, f4.shape[3] - wf - wm), BF16)
-    f_copies = [
-        copy(f4.at[p], frecv.at[d - 1], s_f.at[d - 1], r_f.at[d - 1], (p, j)) for d, p in tms
-    ]
-    for c in f_copies:
-        c.start()
-
-    @pl.loop(0, n_seq)
-    def _(r):
+            f4[a % CORES, a // CORES, b, :, :wf] = facc[b * er : (b + 1) * er, a * wf : (a + 1) * wf].astype(BF16)
+            f4[a % CORES, a // CORES, b, :, wf : wf + wm] = small[b * er : (b + 1) * er, a * wm : (a + 1) * wm].astype(BF16)
+            if wf + wm < f4.shape[4]:
+                f4[a % CORES, a // CORES, b, :, wf + wm :] = jnp.zeros((er, f4.shape[4] - wf - wm), BF16)
+    f_core = copy(f4.at[other], fcore, s_core.at[1], r_core.at[1], sibling)
+    f_core.start()
+
+    def input_gradient(r):
         normed, inv = normalise(r)
         ng = dot(tgs[rows_of(r), :], fw_ref[...], 1, 0) * scale
         m1 = jnp.mean(ng, axis=1, keepdims=True)
         m2 = jnp.mean(ng * normed, axis=1, keepdims=True)
         dx_ref[rows_of(r), :] = (inv * (ng - m1 - normed * m2)).astype(BF16)
 
+    pl.loop(0, n_seq // 2)(input_gradient)
+    f_core.wait()
+    for q in range(chips):
+        fhalf[q] = (f4[core, q].astype(F32) + fcore[q].astype(F32)).astype(BF16)
+    f_copies = [
+        copy(fhalf.at[p], frecv.at[d - 1], s_f.at[d - 1], r_f.at[d - 1], (p * CORES + core, j))
+        for d, p in tms
+    ]
+    for c in f_copies:
+        c.start()
+    pl.loop(n_seq // 2, n_seq)(input_gradient)
+
     for c in w_copies:
         c.wait()
     for b in range(n_seq):
-        total = w4_ref[i, b].astype(F32)
-        for k in range(n_tm - 1):
+        total = whalf[chip, b].astype(F32)
+        for k in range(chips - 1):
             total = total + wrecv[k, b].astype(F32)
         wsum[b] = total.astype(BF16)
     w2_copies = [
@@ -311,8 +332,8 @@
 
     for c in f_copies:
         c.wait()
-    total = f4[i].astype(F32)
-    for k in range(n_tm - 1):
+    total = fhalf[chip].astype(F32)
+    for k in range(chips - 1):
         total = total + frecv[k].astype(F32)
     fsum[...] = total.astype(BF16)
     f2_copies = [
@@ -334,25 +355,30 @@
     total = fsum[j].astype(F32)
     for k in range(n_seq - 1):
         total = total + frecv2[k].astype(F32)
-    gath[i, j] = total.astype(BF16)
+    gath[core, chip, j] = total.astype(BF16)
     g_copies = [
-        copy(gath.at[i, j], gath.at[i, j], s_g.at[d - 1], r_g.at[d - 1], (i, p)) for d, p in seqs
+        copy(gath.at[core, chip, j], gath.at[core, chip, j], s_g.at[d - 1], r_g.at[d - 1], (i, p)) for d, p in seqs
     ]
     for c in g_copies:
         c.start()
     for c in g_copies:
         c.wait()
     g2_copies = [
-        copy(gath.at[i], gath.at[i], s_g2.at[d - 1], r_g2.at[d - 1], (p, j)) for d, p in tms
+        copy(gath.at[core, chip], gath.at[core, chip], s_g2.at[d - 1], r_g2.at[d - 1], (p * CORES + core, j))
+        for d, p in tms
     ]
     for c in g2_copies:
         c.start()
     for c in g2_copies:
         c.wait()
+    g_core = copy(gath.at[core], gath.at[core], s_core.at[2], r_core.at[2], sibling)
+    g_core.start()
+    g_core.wait()
 
 
 def unpack_kernel(gath, wg_ref, fin_ref, mod_ref, in_ref, bias_ref, wg_out, small):
-    n_tm, n_seq, er, _ = gath.shape
+    cores, chips, n_seq, er, _ = gath.shape
+    n_tm = cores * chips
     d_model = fin_ref.shape[1]
     taps_cl, chans = in_ref.shape
     wf = d_model // n_tm
@@ -360,8 +386,8 @@
     pieces = d_model // chans
     for a in range(n_tm):
         for b in range(n_seq):
-            fin_ref[b * er : (b + 1) * er, a * wf : (a + 1) * wf] = gath[a, b, :, :wf].astype(F32)
-            small[b * er : (b + 1) * er, a * wm : (a + 1) * wm] = gath[a, b, :, wf : wf + wm].astype(F32)
+            fin_ref[b * er : (b + 1) * er, a * wf : (a + 1) * wf] = gath[a % cores, a // cores, b, :, :wf].astype(F32)
+            small[b * er : (b + 1) * er, a * wm : (a + 1) * wm] = gath[a % cores, a // cores, b, :, wf : wf + wm].astype(F32)
     in_ref[...] = small[:taps_cl, :]
     bias_ref[...] = small[taps_cl : taps_cl + 1, :]
     for b in range(2):
@@ -376,6 +402,7 @@
     taps, chans = conv_w.shape[:2]
     tokens, d_model = hidden.shape
     rows = chans // (n_tm * n_seq)
+    chips = n_tm // CORES
     backward = [(k, k - 1) for k in range(1, n_tm)]
     forward = [(k, k + 1) for k in range(n_tm - 1)]
     lat_prev = lax.ppermute(latents[slab - 4 :], "tm", forward)
@@ -393,7 +420,7 @@
     ]
     w4 = pl.pallas_call(
         weight_kernel,
-        out_shape=jax.ShapeDtypeStruct((n_tm, n_seq, rows, taps * chans), BF16),
+        out_shape=jax.ShapeDtypeStruct((CORES, chips, n_seq, rows, taps * chans), BF16),
         grid_spec=pltpu.PrefetchScalarGridSpec(
             num_scalar_prefetch=1,
             grid=(slab,),
@@ -404,7 +431,7 @@
                 whole(taps * cl, chans),
                 whole(1, chans),
             ],
-            out_specs=whole(n_tm, n_seq, rows, taps * chans),
+            out_specs=whole(CORES, chips, n_seq, rows, taps * chans),
             scratch_shapes=window
             + [pltpu.VMEM((slab + 2, chans, width), BF16), pltpu.VMEM((chans, taps * chans), F32)],
         ),
@@ -452,13 +479,13 @@
     cw = -(-((d_model + chans) // n_tm) // 128) * 128
     vmem = pl.BlockSpec(memory_space=pltpu.VMEM)
     dma = pltpu.SemaphoreType.DMA
-    nt, ns = n_tm - 1, n_seq - 1
+    nt, ns = chips - 1, n_seq - 1
     dx, wg, gath = pl.pallas_call(
         functools.partial(token_kernel, n_tm, n_seq),
         out_shape=(
             jax.ShapeDtypeStruct((tokens, d_model), BF16),
             jax.ShapeDtypeStruct((taps, rows, chans), F32),
-            jax.ShapeDtypeStruct((n_tm, n_seq, er, cw), BF16),
+            jax.ShapeDtypeStruct((CORES, chips, n_seq, er, cw), BF16),
         ),
         in_specs=[vmem] * 6,
         out_specs=(vmem,) * 3,
@@ -469,10 +496,14 @@
             pltpu.VMEM((e, 128), F32),
             pltpu.VMEM((e, d_model), F32),
             pltpu.VMEM((8, d_model), F32),
+            pltpu.VMEM((chips, n_seq, rows, taps * chans), BF16),
+            pltpu.VMEM((chips, n_seq, rows, taps * chans), BF16),
             pltpu.VMEM((nt, n_seq, rows, taps * chans), BF16),
             pltpu.VMEM((n_seq, rows, taps * chans), BF16),
             pltpu.VMEM((ns, rows, taps * chans), BF16),
-            pltpu.VMEM((n_tm, n_seq, er, cw), BF16),
+            pltpu.VMEM((CORES, chips, n_seq, er, cw), BF16),
+            pltpu.VMEM((chips, n_seq, er, cw), BF16),
+            pltpu.VMEM((chips, n_seq, er, cw), BF16),
             pltpu.VMEM((nt, n_seq, er, cw), BF16),
             pltpu.VMEM((n_seq, er, cw), BF16),
             pltpu.VMEM((ns, er, cw), BF16),
@@ -480,6 +511,7 @@
             dma((nt,)), dma((nt,)), dma((ns,)), dma((ns,)),
             dma((nt,)), dma((nt,)), dma((ns,)), dma((ns,)),
             dma((ns,)), dma((ns,)), dma((nt,)), dma((nt,)),
+            dma((3,)), dma((3,)),
         ],
         compiler_params=pltpu.CompilerParams(
             vmem_limit_bytes=MAX_VMEM, collective_id=0, has_side_effects=True

time: 90.3 us -> 82.1 us (0.909)
  Pallas kernels: 75.1 us -> 66.5 us
    pallas_call x1, Pallas kernels: 52.1 us -> 43.6 us  [local(): pl.pallas_call(functools.partial(token_kernel, n_tm, n_seq), out_shape=(j...]
  transfers between devices with their start and end apart: 2 -> 2, of which waited for: 1 -> 1; matrix products, arithmetic and copies ran while one was open for 0% -> 0% of each run, Pallas kernels for 11% -> 12%
where the time goes in v2:
time: 82.1 us; the launch traced here: 81.9 us
  Pallas kernels  66.5 us (81%)
  local copies, waits for them, and re-layouts  6.65 us (8%)
  starting transfers between devices  6.42 us (8%)
  waiting for transfers between devices  1.63 us (2%)
    pallas_call x1, Pallas kernels, local(): pl.pallas_call(functools.partial(token_kernel, n_tm, n_seq), out_shape=(j...  43.6 us
    pallas_call x1, Pallas kernels, local(): pl.pallas_call(latent_kernel, out_shape=(jax.ShapeDtypeStruct((slab + 2,...  11.3 us
    pallas_call x1, Pallas kernels, local(): pl.pallas_call(weight_kernel, out_shape=jax.ShapeDtypeStruct((CORES, chip...  9.55 us
    unnamed x5, local copies, waits for them, and re-layouts  5.36 us
    ppermute x1, starting transfers between devices, local(): lat_prev = lax.ppermute(latents[slab - 4:], 'tm', forward)  4.49 us
    pallas_call x1, Pallas kernels, local(): pl.pallas_call(unpack_kernel, out_shape=(jax.ShapeDtypeStruct((e, d_model...  2.07 us
    ppermute x1, starting transfers between devices, local(): grad_next = lax.ppermute(grad_out[:2], 'tm', backward)  1.93 us
  transfers between devices with their start and end apart: 2, of which 1 were waited for; matrix products, arithmetic and copies ran while one was open for 0% of the time, Pallas kernels for 12%

profile of v2, /device:TPU:1, one launch (start us, length us, event | category | flops | bytes accessed | tf_op | source)
XLA Modules:
  0.0 81.9 jit_solution(18312352612710193131)
XLA Ops:
  0.6 1.3 %slice.3 = bf16[2,512,512]{2,1,0:T(8,128)(2,1)S(1)} slice(bf16[4,512,512]{2,1,0:T(8,128)(2,1)} %grad_ref.1), slice={[0:2], [0:512], [0:512]} | slice | bytes 2097152 | tf_op jit(solution)/shard_map/slice | solution.py:409
  1.9 1.9 %collective-permute-start.1 = (bf16[2,512,512]{2,1,0:T(8,128)(2,1)S(1)}, bf16[2,512,512]{2,1,0:T(8,128)(2,1)S(1)}, u32[]{:S(2)}, u32[]{:S(2)}) collective-permute-start(bf16[2,512,512]{2,1,0:T(8,128)(2,1)S(1)} %slice.3), channel_id=1, source_target_pairs={{4,0},{8,4},{12,8},{16,12},{20,16},{24,20},{28,24},{5,1},{9,5},{13... | collective-permute-start | bytes 3145736 | tf_op jit(solution)/shard_map/ppermute | solution.py:409
  3.9 4.5 %collective-permute-start = (bf16[4,16,512]{2,1,0:T(8,128)(2,1)}, bf16[4,16,512]{2,1,0:T(8,128)(2,1)S(1)}, u32[]{:S(2)}, u32[]{:S(2)}) collective-permute-start(bf16[4,16,512]{2,1,0:T(8,128)(2,1)} %lat_ref.3), channel_id=1, source_target_pairs={{0,4},{4,8},{8,12},{12,16},{16,20},{20,24},{24,28},{1,5},{5,9},{9,... | collective-permute-start | bytes 196616 | tf_op jit(solution)/shard_map/ppermute | solution.py:408
  8.4 1.6 %collective-permute-done.prev_ref = bf16[4,16,512]{2,1,0:T(8,128)(2,1)S(1)} collective-permute-done((bf16[4,16,512]{2,1,0:T(8,128)(2,1)}, bf16[4,16,512]{2,1,0:T(8,128)(2,1)S(1)}, u32[]{:S(2)}, u32[]{:S(2)}) %collective-permute-start) | collective-permute-done | bytes 65568 | tf_op jit(solution)/shard_map/ppermute | solution.py:408
  10.0 0.0 copy-start.1
  10.0 0.6 copy-done.1
  10.6 9.6 %weight_grad.1.w4_ref = bf16[2,4,4,16,1536]{4,3,2,1,0:T(8,128)(2,1)} custom-call(s32[32]{0:T(128)} %clip_ref.3, bf16[4,16,512]{2,1,0:T(8,128)(2,1)} %copy-done.1, bf16[4,16,512]{2,1,0:T(8,128)(2,1)} %lat_ref.3, bf16[4,512,512]{2,1,0:T(8,128)(2,1)} %grad_ref.1, bf16[48,512]{1,0:T(8,128)(2,1)} %bitcast.19, f32[1,512]{1,0:T(1,128)} %bitcast.21), custom_call_target="tpu_custom_call" | custom-call | flops 7000000000 | bytes 6000000 | tf_op jit(solution)/shard_map/weight_grad/pallas_call | solution.py:421
  20.2 0.0 collective-permute-done.1
  20.2 0.0 copy-start
  20.2 1.0 %copy-done = bf16[2,512,512]{2,1,0:T(8,128)(2,1)} copy-done((bf16[2,512,512]{2,1,0:T(8,128)(2,1)}, bf16[2,512,512]{2,1,0:T(8,128)(2,1)S(1)}, u32[]{:S(2)}) %copy-start) | copy-done | bytes 1048600
  21.1 11.3 %latent_grad.1 = (f32[6,16,512]{2,1,0:T(8,128)}, f32[64,512]{1,0:T(8,128)}) custom-call(s32[32]{0:T(128)} %clip_ref.3, bf16[4,16,512]{2,1,0:T(8,128)(2,1)} %copy-done.1, bf16[4,16,512]{2,1,0:T(8,128)(2,1)} %lat_ref.3, bf16[2048,512]{1,0:T(8,128)(2,1)} %bitcast.13, bf16[1024,512]{1,0:T(8,128)(2,1)} %bitcast.15, bf16[48,512]{1,0:T(8,128)(2,1)} %bitcast.20, ...), custom_call_target="tpu_custom_call" | custom-call | flops 7000000000 | bytes 6000000 | tf_op jit(solution)/shard_map/latent_grad/pallas_call | solution.py:443
  32.5 43.6 %token_grad.1 = (bf16[512,3072]{1,0:T(8,128)(2,1)}, f32[3,16,512]{2,1,0:T(8,128)}, bf16[2,4,4,16,512]{4,3,2,1,0:T(8,128)(2,1)}) custom-call(f32[6,16,512]{2,1,0:T(8,128)} %get-tuple-element.16.lg_ref, bf16[512,3072]{1,0:T(8,128)(2,1)} %hid_ref.1, bf16[64,3072]{1,0:T(8,128)(2,1)} %bitcast.14, f32[2,3072]{1,0:T(2,128)} %modu_ref.1, ...), custom_call_target="tpu_custom_call" | custom-call | tf_op jit(solution)/shard_map/token_grad/pallas_call | solution.py:483
  76.1 2.1 %unpack.1 = (f32[64,3072]{1,0:T(8,128)}, f32[2,3072]{1,0:T(2,128)}, f32[48,512]{1,0:T(8,128)}, f32[1,512]{1,0:T(1,128)}, f32[3,16,512]{2,1,0:T(8,128)}) custom-call(bf16[2,4,4,16,512]{4,3,2,1,0:T(8,128)(2,1)} %get-tuple-element.19.gath, f32[3,16,512]{2,1,0:T(8,128)} %get-tuple-element.20.wg_ref), custom_call_target="tpu_custom_call" | custom-call | tf_op jit(solution)/shard_map/unpack/pallas_call | solution.py:521
  78.1 3.8 %copy.16 = bf16[512,3072]{1,0:T(8,128)(2,1)} copy(bf16[512,3072]{1,0:T(8,128)(2,1)} %get-tuple-element.32) | data formatting | bytes 6291456
Async XLA Ops:
  1.9 18.2 %collective-permute-start.1 = (bf16[2,512,512]{2,1,0:T(8,128)(2,1)S(1)}, bf16[2,512,512]{2,1,0:T(8,128)(2,1)S(1)}, u32[]{:S(2)}, u32[]{:S(2)}) collective-permute-start(bf16[2,512,512]{2,1,0:T(8,128)(2,1)S(1)} %slice.3), channel_id=1, source_target_pairs={{4,0},{8,4},{12,8},{16,12},{20,16},{24,20},{28,24},{5,1},{9,5},{13... | collective-permute-start | bytes 3145736 | tf_op jit(solution)/shard_map/ppermute | solution.py:409
  3.9 6.1 %collective-permute-start = (bf16[4,16,512]{2,1,0:T(8,128)(2,1)}, bf16[4,16,512]{2,1,0:T(8,128)(2,1)S(1)}, u32[]{:S(2)}, u32[]{:S(2)}) collective-permute-start(bf16[4,16,512]{2,1,0:T(8,128)(2,1)} %lat_ref.3), channel_id=1, source_target_pairs={{0,4},{4,8},{8,12},{12,16},{16,20},{20,24},{24,28},{1,5},{5,9},{9,... | collective-permute-start | bytes 196616 | tf_op jit(solution)/shard_map/ppermute | solution.py:408
  10.0 0.6 copy-start.1
  20.2 1.0 %copy-start = (bf16[2,512,512]{2,1,0:T(8,128)(2,1)}, bf16[2,512,512]{2,1,0:T(8,128)(2,1)S(1)}, u32[]{:S(2)}) copy-start(bf16[2,512,512]{2,1,0:T(8,128)(2,1)S(1)} %collective-permute-done.1) | copy-start | bytes 3145732

commit v3 on v2

--- a/solution.py
+++ b/solution.py
@@ -154,9 +154,9 @@
 
 def token_kernel(
     n_tm, n_seq,
-    lg_ref, hid_ref, fw_ref, modu_ref, w4_ref, misc_ref,
-    dx_ref, wg_ref, gath,
-    tok, tok_halo, tgs, tcol, facc, macc, wcore, whalf, wrecv, wsum, wrecv2, f4, fcore, fhalf, frecv, fsum, frecv2,
+    lg_ref, hid_hbm, fw_ref, modu_ref, w4_ref, misc_ref,
+    dx_hbm, wg_ref, gath,
+    hid_ref, dx_ref, s_hid, s_dx, tok, tok_halo, tgs, tcol, facc, macc, wcore, whalf, wrecv, wsum, wrecv2, f4, fcore, fhalf, frecv, fsum, frecv2,
     s_tok, r_tok, s_halo, r_halo, s_w, r_w, s_w2, r_w2, s_f, r_f, s_f2, r_f2, s_g, r_g, s_g2, r_g2, s_core, r_core,
 ):
     i = lax.axis_index("tm")
@@ -171,6 +171,8 @@
     cl = lg_ref.shape[1]
     width = lg_ref.shape[2]
     d_model = hid_ref.shape[1]
+    hid_copy = pltpu.make_async_copy(hid_hbm, hid_ref, s_hid)
+    hid_copy.start()
     takes_halo = (i < n_tm - 1) & (j >= n_seq - 2)
 
     barrier = pltpu.get_barrier_semaphore()
@@ -260,6 +262,8 @@
         center = hid - jnp.mean(hid, axis=1, keepdims=True)
         inv = lax.rsqrt(jnp.mean(center * center, axis=1, keepdims=True) + 1e-06)
         return center * inv, inv
+
+    hid_copy.wait()
 
     @pl.loop(0, n_seq)
     def _(r):
@@ -316,6 +320,8 @@
     for c in f_copies:
         c.start()
     pl.loop(n_seq // 2, n_seq)(input_gradient)
+    dx_copy = pltpu.make_async_copy(dx_ref, dx_hbm, s_dx)
+    dx_copy.start()
 
     for c in w_copies:
         c.wait()
@@ -374,6 +380,7 @@
     g_core = copy(gath.at[core], gath.at[core], s_core.at[2], r_core.at[2], sibling)
     g_core.start()
     g_core.wait()
+    dx_copy.wait()
 
 
 def unpack_kernel(gath, wg_ref, fin_ref, mod_ref, in_ref, bias_ref, wg_out, small):
@@ -487,9 +494,13 @@
             jax.ShapeDtypeStruct((taps, rows, chans), F32),
             jax.ShapeDtypeStruct((CORES, chips, n_seq, er, cw), BF16),
         ),
-        in_specs=[vmem] * 6,
-        out_specs=(vmem,) * 3,
+        in_specs=[vmem, pl.BlockSpec(memory_space=pl.ANY)] + [vmem] * 4,
+        out_specs=(pl.BlockSpec(memory_space=pl.ANY), vmem, vmem),
         scratch_shapes=[
+            pltpu.VMEM((tokens, d_model), BF16),
+            pltpu.VMEM((tokens, d_model), BF16),
+            dma(()),
+            dma(()),
             pltpu.VMEM((n_seq, cl, width), F32),
             pltpu.VMEM((n_seq, cl, width), F32),
             pltpu.VMEM((tokens, e), BF16),

time: 82.1 us -> 80.2 us (0.977)
  Pallas kernels: 66.5 us -> 64.3 us
    pallas_call x1, Pallas kernels: 43.6 us -> 41.4 us  [local(): pl.pallas_call(functools.partial(token_kernel, n_tm, n_seq), out_shape=(j...]
where the time goes in v3:
time: 80.2 us; the launch traced here: 79.7 us
  Pallas kernels  64.3 us (80%)
  local copies, waits for them, and re-layouts  6.65 us (8%)
  starting transfers between devices  6.42 us (8%)
  waiting for transfers between devices  1.63 us (2%)
    pallas_call x1, Pallas kernels, local(): pl.pallas_call(functools.partial(token_kernel, n_tm, n_seq), out_shape=(j...  41.4 us
    pallas_call x1, Pallas kernels, local(): pl.pallas_call(latent_kernel, out_shape=(jax.ShapeDtypeStruct((slab + 2,...  11.3 us
    pallas_call x1, Pallas kernels, local(): pl.pallas_call(weight_kernel, out_shape=jax.ShapeDtypeStruct((CORES, chip...  9.55 us
    unnamed x5, local copies, waits for them, and re-layouts  5.36 us
    ppermute x1, starting transfers between devices, local(): lat_prev = lax.ppermute(latents[slab - 4:], 'tm', forward)  4.49 us
    pallas_call x1, Pallas kernels, local(): pl.pallas_call(unpack_kernel, out_shape=(jax.ShapeDtypeStruct((e, d_model...  2.07 us
    ppermute x1, starting transfers between devices, local(): grad_next = lax.ppermute(grad_out[:2], 'tm', backward)  1.93 us
    ppermute x1, waiting for transfers between devices, local(): lat_prev = lax.ppermute(latents[slab - 4:], 'tm', forward)  1.63 us
  transfers between devices with their start and end apart: 2, of which 1 were waited for; matrix products, arithmetic and copies ran while one was open for 0% of the time, Pallas kernels for 12%

profile of v3, /device:TPU:1, one launch (start us, length us, event | category | flops | bytes accessed | tf_op | source)
XLA Modules:
  0.0 79.7 jit_solution(7585962433673376044)
XLA Ops:
  0.6 1.3 %slice.3 = bf16[2,512,512]{2,1,0:T(8,128)(2,1)S(1)} slice(bf16[4,512,512]{2,1,0:T(8,128)(2,1)} %grad_ref.1), slice={[0:2], [0:512], [0:512]} | slice | bytes 2097152 | tf_op jit(solution)/shard_map/slice | solution.py:416
  1.9 1.9 %collective-permute-start.1 = (bf16[2,512,512]{2,1,0:T(8,128)(2,1)S(1)}, bf16[2,512,512]{2,1,0:T(8,128)(2,1)S(1)}, u32[]{:S(2)}, u32[]{:S(2)}) collective-permute-start(bf16[2,512,512]{2,1,0:T(8,128)(2,1)S(1)} %slice.3), channel_id=1, source_target_pairs={{4,0},{8,4},{12,8},{16,12},{20,16},{24,20},{28,24},{5,1},{9,5},{13... | collective-permute-start | bytes 3145736 | tf_op jit(solution)/shard_map/ppermute | solution.py:416
  3.9 4.5 %collective-permute-start = (bf16[4,16,512]{2,1,0:T(8,128)(2,1)}, bf16[4,16,512]{2,1,0:T(8,128)(2,1)S(1)}, u32[]{:S(2)}, u32[]{:S(2)}) collective-permute-start(bf16[4,16,512]{2,1,0:T(8,128)(2,1)} %lat_ref.3), channel_id=1, source_target_pairs={{0,4},{4,8},{8,12},{12,16},{16,20},{20,24},{24,28},{1,5},{5,9},{9,... | collective-permute-start | bytes 196616 | tf_op jit(solution)/shard_map/ppermute | solution.py:415
  8.4 1.6 %collective-permute-done.prev_ref = bf16[4,16,512]{2,1,0:T(8,128)(2,1)S(1)} collective-permute-done((bf16[4,16,512]{2,1,0:T(8,128)(2,1)}, bf16[4,16,512]{2,1,0:T(8,128)(2,1)S(1)}, u32[]{:S(2)}, u32[]{:S(2)}) %collective-permute-start) | collective-permute-done | bytes 65568 | tf_op jit(solution)/shard_map/ppermute | solution.py:415
  10.0 0.0 copy-start.1
  10.0 0.6 copy-done.1
  10.6 9.6 %weight_grad.1.w4_ref = bf16[2,4,4,16,1536]{4,3,2,1,0:T(8,128)(2,1)} custom-call(s32[32]{0:T(128)} %clip_ref.3, bf16[4,16,512]{2,1,0:T(8,128)(2,1)} %copy-done.1, bf16[4,16,512]{2,1,0:T(8,128)(2,1)} %lat_ref.3, bf16[4,512,512]{2,1,0:T(8,128)(2,1)} %grad_ref.1, bf16[48,512]{1,0:T(8,128)(2,1)} %bitcast.19, f32[1,512]{1,0:T(1,128)} %bitcast.21), custom_call_target="tpu_custom_call" | custom-call | flops 7000000000 | bytes 6000000 | tf_op jit(solution)/shard_map/weight_grad/pallas_call | solution.py:428
  20.2 0.0 collective-permute-done.1
  20.2 0.0 copy-start
  20.2 1.0 %copy-done = bf16[2,512,512]{2,1,0:T(8,128)(2,1)} copy-done((bf16[2,512,512]{2,1,0:T(8,128)(2,1)}, bf16[2,512,512]{2,1,0:T(8,128)(2,1)S(1)}, u32[]{:S(2)}) %copy-start) | copy-done | bytes 1048600
  21.1 11.3 %latent_grad.1 = (f32[6,16,512]{2,1,0:T(8,128)}, f32[64,512]{1,0:T(8,128)}) custom-call(s32[32]{0:T(128)} %clip_ref.3, bf16[4,16,512]{2,1,0:T(8,128)(2,1)} %copy-done.1, bf16[4,16,512]{2,1,0:T(8,128)(2,1)} %lat_ref.3, bf16[2048,512]{1,0:T(8,128)(2,1)} %bitcast.13, bf16[1024,512]{1,0:T(8,128)(2,1)} %bitcast.15, bf16[48,512]{1,0:T(8,128)(2,1)} %bitcast.20, ...), custom_call_target="tpu_custom_call" | custom-call | flops 7000000000 | bytes 6000000 | tf_op jit(solution)/shard_map/latent_grad/pallas_call | solution.py:450
  32.5 41.4 %token_grad.1 = (bf16[512,3072]{1,0:T(8,128)(2,1)}, f32[3,16,512]{2,1,0:T(8,128)}, bf16[2,4,4,16,512]{4,3,2,1,0:T(8,128)(2,1)}) custom-call(f32[6,16,512]{2,1,0:T(8,128)} %get-tuple-element.16.lg_ref, bf16[512,3072]{1,0:T(8,128)(2,1)} %hid_hbm.1, bf16[64,3072]{1,0:T(8,128)(2,1)} %bitcast.14, f32[2,3072]{1,0:T(2,128)} %modu_ref.1, ...), custom_call_target="tpu_custom_call" | custom-call | tf_op jit(solution)/shard_map/token_grad/pallas_call | solution.py:490
  73.9 2.1 %unpack.1 = (f32[64,3072]{1,0:T(8,128)}, f32[2,3072]{1,0:T(2,128)}, f32[48,512]{1,0:T(8,128)}, f32[1,512]{1,0:T(1,128)}, f32[3,16,512]{2,1,0:T(8,128)}) custom-call(bf16[2,4,4,16,512]{4,3,2,1,0:T(8,128)(2,1)} %get-tuple-element.19.gath, f32[3,16,512]{2,1,0:T(8,128)} %get-tuple-element.20.wg_ref), custom_call_target="tpu_custom_call" | custom-call | tf_op jit(solution)/shard_map/unpack/pallas_call | solution.py:532
  75.9 3.8 %copy.16 = bf16[512,3072]{1,0:T(8,128)(2,1)} copy(bf16[512,3072]{1,0:T(8,128)(2,1)} %get-tuple-element.32) | data formatting | bytes 6291456
Async XLA Ops:
  1.9 18.2 %collective-permute-start.1 = (bf16[2,512,512]{2,1,0:T(8,128)(2,1)S(1)}, bf16[2,512,512]{2,1,0:T(8,128)(2,1)S(1)}, u32[]{:S(2)}, u32[]{:S(2)}) collective-permute-start(bf16[2,512,512]{2,1,0:T(8,128)(2,1)S(1)} %slice.3), channel_id=1, source_target_pairs={{4,0},{8,4},{12,8},{16,12},{20,16},{24,20},{28,24},{5,1},{9,5},{13... | collective-permute-start | bytes 3145736 | tf_op jit(solution)/shard_map/ppermute | solution.py:416
  3.9 6.1 %collective-permute-start = (bf16[4,16,512]{2,1,0:T(8,128)(2,1)}, bf16[4,16,512]{2,1,0:T(8,128)(2,1)S(1)}, u32[]{:S(2)}, u32[]{:S(2)}) collective-permute-start(bf16[4,16,512]{2,1,0:T(8,128)(2,1)} %lat_ref.3), channel_id=1, source_target_pairs={{0,4},{4,8},{8,12},{12,16},{16,20},{20,24},{24,28},{1,5},{5,9},{9,... | collective-permute-start | bytes 196616 | tf_op jit(solution)/shard_map/ppermute | solution.py:415
  10.0 0.6 copy-start.1
  20.2 1.0 %copy-start = (bf16[2,512,512]{2,1,0:T(8,128)(2,1)}, bf16[2,512,512]{2,1,0:T(8,128)(2,1)S(1)}, u32[]{:S(2)}) copy-start(bf16[2,512,512]{2,1,0:T(8,128)(2,1)S(1)} %collective-permute-done.1) | copy-start | bytes 3145732
